TPU v7x, 32 devices: a whole 2x2x4 slice. The times are simulated.
32 devices in a mesh: dp: 8 (over z, y), inner: 4 (over x, core).
Axes of the slice: x: 2, y: 2, z: 4, core: 2. Of those that a mesh axis runs over, the one named last changes fastest.
Arguments:
- tokens: bfloat16 [32768, 512], P(('dp', 'inner')), may hold values from -6 to 6
- segments: int32 [32768], P(('dp', 'inner')), may hold values from 0 to 32767, as said below
- positions: int32 [32768], P(('dp', 'inner')), may hold values from 0 to 1023, as said below
- cotangent: bfloat16 [32768, 512], P(('dp', 'inner')), may hold values from -6 to 6
- attn_weight: float32 [4, 512, 512], P(None, ('dp', 'inner')), may hold values from -0.53033009 to 0.53033009
- attn_m: float32 [4, 512, 512], P(None, ('dp', 'inner')), may hold values from -0.0007324219 to 0.0007324219
- attn_v: float32 [4, 512, 512], P(None, ('dp', 'inner')), may hold values from 1.0882435e-09 to 4.352974e-09
- gate_weight: float32 [2, 512, 512], P(None, ('dp', 'inner')), may hold values from -0.25 to 0.25
- gate_m: float32 [2, 512, 512], P(None, ('dp', 'inner')), may hold values from -0.00036621094 to 0.00036621094
- gate_v: float32 [2, 512, 512], P(None, ('dp', 'inner')), may hold values from 2.7206087e-10 to 1.0882435e-09
- in_weight: float32 [512, 2048], P(('dp', 'inner')), may hold values from -0.25 to 0.25
- in_m: float32 [512, 2048], P(('dp', 'inner')), may hold values from -0.00036621094 to 0.00036621094
- in_v: float32 [512, 2048], P(('dp', 'inner')), may hold values from 2.7206087e-10 to 1.0882435e-09
- out_weight: float32 [2048, 512], P(('dp', 'inner')), may hold values from -0.125 to 0.125
- out_m: float32 [2048, 512], P(('dp', 'inner')), may hold values from -0.00036621094 to 0.00036621094
- out_v: float32 [2048, 512], P(('dp', 'inner')), may hold values from 2.7206087e-10 to 1.0882435e-09
- norm_params: float32 [7, 512], P(None, ('dp', 'inner'))
- norm_m: float32 [7, 512], P(None, ('dp', 'inner')), may hold values from -0.0014648438 to 0.0014648438
- norm_v: float32 [7, 512], P(None, ('dp', 'inner')), may hold values from 4.352974e-09 to 1.7411896e-08
- in_bias: float32 [2048], P(('dp', 'inner')), may hold values from -1.75 to 1.75
- bias_m: float32 [2048], P(('dp', 'inner')), may hold values from -0.00024414062 to 0.00024414062
- bias_v: float32 [2048], P(('dp', 'inner')), may hold values from 1.7411896e-10 to 7.073583e-10
Outputs:
- layer_out: bfloat16 [32768, 512], P(('dp', 'inner'))
- input_grad: bfloat16 [32768, 512], P(('dp', 'inner'))
- grad_norm: float32 [], replicated
- attn_new: float32 [4, 512, 512], P(None, ('dp', 'inner'))
- attn_m_new: float32 [4, 512, 512], P(None, ('dp', 'inner'))
- attn_v_new: float32 [4, 512, 512], P(None, ('dp', 'inner'))
- gate_new: float32 [2, 512, 512], P(None, ('dp', 'inner'))
- gate_m_new: float32 [2, 512, 512], P(None, ('dp', 'inner'))
- gate_v_new: float32 [2, 512, 512], P(None, ('dp', 'inner'))
- in_new: float32 [512, 2048], P(('dp', 'inner'))
- in_m_new: float32 [512, 2048], P(('dp', 'inner'))
- in_v_new: float32 [512, 2048], P(('dp', 'inner'))
- out_new: float32 [2048, 512], P(('dp', 'inner'))
- out_m_new: float32 [2048, 512], P(('dp', 'inner'))
- out_v_new: float32 [2048, 512], P(('dp', 'inner'))
- norm_new: float32 [7, 512], P(None, ('dp', 'inner'))
- norm_m_new: float32 [7, 512], P(None, ('dp', 'inner'))
- norm_v_new: float32 [7, 512], P(None, ('dp', 'inner'))
- bias_new: float32 [2048], P(('dp', 'inner'))
- bias_m_new: float32 [2048], P(('dp', 'inner'))
- bias_v_new: float32 [2048], P(('dp', 'inner'))
Inputs may be any that keep to these rules, and one draw needn't show every extreme that they name: `segments`: a token's segment number is the index of its document's first token, so segment numbers never fall; a new document begins at every sequence start (every 1024 tokens); the first sequence is one document; the last token forms a document of its own. positions restart at 0 with every new segment number.
All inputs are finite; a program needn't handle non-finite values.
Results may differ from a plain program's by a relative error of at most 0.033.
The roundings to bfloat16 on the way count: a program that leaves them out, or rounds other values in their place, can miss the bound.
Values may be sent and summed in bfloat16 or wider, within the bound.
No kernel may reach another device: no remote copies, remote signals or barrier semaphores. Data moves between devices by JAX's collectives and lax.ppermute only.
A program may use at most 192 MiB of HBM per device.

v0:
```python
import jax
import jax.numpy as jnp
from jax import lax
from jax.sharding import PartitionSpec as P

HEADS = 8
HEAD = 64
STEP = 10
norm_eps = 1e-05
first_decay = 0.9
second_decay = 0.999
adam_eps = 1e-08
learn_rate = 0.05
vector_rate = 0.8
weight_decay = 0.1
clip_norm = 1.0
masked_score = -1e30


def normalize_parts(values, gain_row, bias_row):
    centred = values - jnp.mean(values, -1, keepdims=True)
    spread = jnp.mean(centred * centred, -1, keepdims=True)
    scale_row = lax.rsqrt(spread + norm_eps)
    unit_rows = centred * scale_row
    return (unit_rows * gain_row + bias_row, unit_rows, scale_row)


def normalize_back(grad_rows, unit_rows, scale_row, gain_row):
    grad_unit = grad_rows * gain_row
    return scale_row * (
        grad_unit
        - jnp.mean(grad_unit, -1, keepdims=True)
        - unit_rows * jnp.mean(grad_unit * unit_rows, -1, keepdims=True)
    )


def fetch(shards):
    low_attn, low_gate, low_in, low_out, low_vec, low_shift = [
        element.astype(jnp.bfloat16) for element in shards
    ]
    return (
        lax.all_gather(low_attn, ("dp", "inner"), axis=1, tiled=True),
        lax.all_gather(low_gate, ("dp", "inner"), axis=1, tiled=True),
        lax.all_gather(low_in, ("dp", "inner"), axis=0, tiled=True),
        lax.all_gather(low_out, ("dp", "inner"), axis=0, tiled=True),
        lax.all_gather(low_vec, ("dp", "inner"), axis=1, tiled=True),
        lax.all_gather(low_shift, ("dp", "inner"), axis=0, tiled=True),
    )


def score_block(queries, key_heads, segments, positions, first_row, block_size):
    query_part = lax.slice_in_dim(queries, first_row, first_row + block_size, axis=0)
    raw_scores = jnp.einsum(
        "qhe,khe->hqk", query_part, key_heads, preferred_element_type=jnp.float32
    )
    own_segments = lax.slice_in_dim(segments, first_row, first_row + block_size, axis=0)
    own_positions = lax.slice_in_dim(positions, first_row, first_row + block_size, axis=0)
    allowed = (own_segments[:, None] == segments[None, :]) & (
        positions[None, :] <= own_positions[:, None]
    )
    return (jnp.where(allowed[None], raw_scores * HEAD ** (-0.5), masked_score), query_part)


def attend(triple, segments, positions):
    row_count = triple.shape[1]
    block_size = min(512, row_count)
    queries = triple[0].reshape(row_count, HEADS, HEAD)
    key_heads = triple[1].reshape(row_count, HEADS, HEAD)
    value_heads = triple[2].reshape(row_count, HEADS, HEAD)
    mixed_parts = []
    total_parts = []
    for first_row in range(0, row_count, block_size):
        scores, query_part = score_block(
            queries, key_heads, segments, positions, first_row, block_size
        )
        row_max = jnp.max(scores, -1, keepdims=True)
        weights = jnp.exp(scores - row_max)
        exp_total = jnp.sum(weights, -1, keepdims=True)
        attn_probs = (weights / exp_total).astype(jnp.bfloat16)
        mixed_block = jnp.einsum(
            "hqk,khe->qhe", attn_probs, value_heads, preferred_element_type=jnp.float32
        )
        mixed_parts.append(mixed_block.reshape(block_size, HEADS * HEAD))
        total_parts.append(row_max + jnp.log(exp_total))
    mixed_heads = jnp.concatenate(mixed_parts, 0).astype(jnp.bfloat16)
    return (mixed_heads, jnp.concatenate(total_parts, 1))


def attend_back(triple, grad_mixed, log_total, segments, positions):
    row_count = triple.shape[1]
    block_size = min(512, row_count)
    queries = triple[0].reshape(row_count, HEADS, HEAD)
    key_heads = triple[1].reshape(row_count, HEADS, HEAD)
    value_heads = triple[2].reshape(row_count, HEADS, HEAD)
    grad_heads = grad_mixed.reshape(row_count, HEADS, HEAD)
    query_grads = []
    grad_keys = jnp.zeros((row_count, HEADS, HEAD), jnp.float32)
    grad_values = jnp.zeros((row_count, HEADS, HEAD), jnp.float32)
    for first_row in range(0, row_count, block_size):
        scores, query_part = score_block(
            queries, key_heads, segments, positions, first_row, block_size
        )
        attn_probs = jnp.exp(
            scores - lax.slice_in_dim(log_total, first_row, first_row + block_size, axis=1)
        )
        grad_part = lax.slice_in_dim(grad_heads, first_row, first_row + block_size, axis=0)
        grad_probs = jnp.einsum(
            "qhe,khe->hqk", grad_part, value_heads, preferred_element_type=jnp.float32
        )
        row_inner = jnp.sum(attn_probs * grad_probs, -1, keepdims=True)
        grad_raw = (attn_probs * (grad_probs - row_inner) * HEAD ** (-0.5)).astype(jnp.bfloat16)
        query_grads.append(
            jnp.einsum(
                "hqk,khe->qhe", grad_raw, key_heads, preferred_element_type=jnp.float32
            ).reshape(block_size, HEADS * HEAD)
        )
        grad_keys = grad_keys + jnp.einsum(
            "hqk,qhe->khe", grad_raw, query_part, preferred_element_type=jnp.float32
        )
        grad_values = grad_values + jnp.einsum(
            "hqk,qhe->khe",
            attn_probs.astype(jnp.bfloat16),
            grad_part,
            preferred_element_type=jnp.float32,
        )
    grad_query_rows = jnp.concatenate(query_grads, 0)
    stacked = jnp.stack(
        [
            grad_query_rows,
            grad_keys.reshape(row_count, HEADS * HEAD),
            grad_values.reshape(row_count, HEADS * HEAD),
        ]
    )
    return stacked.astype(jnp.bfloat16)


def attn_branch(weights, normed, segments, positions):
    triple = jnp.einsum(
        "td,jde->jte", normed, weights[0][:3], preferred_element_type=jnp.float32
    ).astype(jnp.bfloat16)
    mixed_heads, log_total = attend(triple, segments, positions)
    attended = jnp.dot(mixed_heads, weights[0][3], preferred_element_type=jnp.float32)
    return (triple, mixed_heads, log_total, attended)


def ffn_branch(weights, normed_two):
    hidden = jnp.dot(normed_two, weights[2], preferred_element_type=jnp.float32) + weights[
        5
    ].astype(jnp.float32)
    active = jnp.maximum(hidden, 0.0).astype(jnp.bfloat16)
    branch = jnp.dot(active, weights[3], preferred_element_type=jnp.float32) + weights[4][6].astype(
        jnp.float32
    )
    return (hidden, active, branch)


def adam_update(weight, first_moment, second_moment, gradient, factor, step_rate):
    clipped = gradient * factor
    first_new = first_decay * first_moment + (1.0 - first_decay) * clipped
    second_new = second_decay * second_moment + (1.0 - second_decay) * clipped * clipped
    corrected = first_new / (1.0 - first_decay**STEP)
    spread = second_new / (1.0 - second_decay**STEP)
    weight_new = weight - step_rate * (
        corrected / (jnp.sqrt(spread) + adam_eps) + weight_decay * weight
    )
    return (weight_new, first_new, second_new)


def body(
    tokens,
    segments,
    positions,
    cotangent,
    attn_weight,
    attn_m,
    attn_v,
    gate_weight,
    gate_m,
    gate_v,
    in_weight,
    in_m,
    in_v,
    out_weight,
    out_m,
    out_v,
    norm_params,
    norm_m,
    norm_v,
    in_bias,
    bias_m,
    bias_v,
):
    shards = (attn_weight, gate_weight, in_weight, out_weight, norm_params, in_bias)
    weights = fetch(shards)
    vectors = weights[4].astype(jnp.float32)
    inputs = tokens.astype(jnp.float32)
    normed_full, unit_one, scale_one = normalize_parts(inputs, vectors[0], vectors[1])
    normed = normed_full.astype(jnp.bfloat16)
    triple, mixed_heads, log_total, attended = attn_branch(weights, normed, segments, positions)
    attn_gate = jax.nn.sigmoid(
        jnp.dot(normed, weights[1][0], preferred_element_type=jnp.float32) + vectors[4]
    )
    middle = attn_gate * attended + (1.0 - attn_gate) * inputs
    normed_two_full, unit_two, scale_two = normalize_parts(middle, vectors[2], vectors[3])
    normed_two = normed_two_full.astype(jnp.bfloat16)
    hidden, active, branch = ffn_branch(weights, normed_two)
    ffn_gate = jax.nn.sigmoid(
        jnp.dot(normed_two, weights[1][1], preferred_element_type=jnp.float32) + vectors[5]
    )
    layer_out = (ffn_gate * branch + (1.0 - ffn_gate) * middle).astype(jnp.bfloat16)
    weights = fetch(shards)
    triple, mixed_heads, log_total, attended = attn_branch(weights, normed, segments, positions)
    hidden, active, branch = ffn_branch(weights, normed_two)
    grad_out = cotangent.astype(jnp.float32)
    grad_branch = grad_out * ffn_gate
    grad_fgate = grad_out * (branch - middle) * ffn_gate * (1.0 - ffn_gate)
    grad_middle = grad_out * (1.0 - ffn_gate)
    branch_low = grad_branch.astype(jnp.bfloat16)
    grad_w_out = jnp.einsum("tf,td->fd", active, branch_low, preferred_element_type=jnp.float32)
    grad_active = jnp.einsum(
        "td,fd->tf", branch_low, weights[3], preferred_element_type=jnp.float32
    )
    grad_hidden = jnp.where(hidden > 0.0, grad_active, 0.0)
    hidden_low = grad_hidden.astype(jnp.bfloat16)
    grad_w_in = jnp.einsum("td,tf->df", normed_two, hidden_low, preferred_element_type=jnp.float32)
    fgate_low = grad_fgate.astype(jnp.bfloat16)
    grad_w_fgate = jnp.einsum(
        "td,te->de", normed_two, fgate_low, preferred_element_type=jnp.float32
    )
    grad_normed_two = jnp.einsum(
        "tf,df->td", hidden_low, weights[2], preferred_element_type=jnp.float32
    )
    grad_normed_two = grad_normed_two + jnp.einsum(
        "te,de->td", fgate_low, weights[1][1], preferred_element_type=jnp.float32
    )
    grad_gain_two = jnp.sum(grad_normed_two * unit_two, 0)
    grad_shift_two = jnp.sum(grad_normed_two, 0)
    grad_middle = grad_middle + normalize_back(grad_normed_two, unit_two, scale_two, vectors[2])
    grad_attended = grad_middle * attn_gate
    grad_agate = grad_middle * (attended - inputs) * attn_gate * (1.0 - attn_gate)
    grad_inputs = grad_middle * (1.0 - attn_gate)
    attended_low = grad_attended.astype(jnp.bfloat16)
    grad_w_o = jnp.einsum(
        "td,te->de", mixed_heads, attended_low, preferred_element_type=jnp.float32
    )
    grad_mixed = jnp.einsum(
        "te,de->td", attended_low, weights[0][3], preferred_element_type=jnp.float32
    ).astype(jnp.bfloat16)
    triple_grad = attend_back(triple, grad_mixed, log_total, segments, positions)
    grad_w_qkv = jnp.einsum("td,jte->jde", normed, triple_grad, preferred_element_type=jnp.float32)
    agate_low = grad_agate.astype(jnp.bfloat16)
    grad_w_agate = jnp.einsum("td,te->de", normed, agate_low, preferred_element_type=jnp.float32)
    grad_normed = jnp.einsum(
        "jte,jde->td", triple_grad, weights[0][:3], preferred_element_type=jnp.float32
    )
    grad_normed = grad_normed + jnp.einsum(
        "te,de->td", agate_low, weights[1][0], preferred_element_type=jnp.float32
    )
    grad_gain_one = jnp.sum(grad_normed * unit_one, 0)
    grad_shift_one = jnp.sum(grad_normed, 0)
    grad_inputs = grad_inputs + normalize_back(grad_normed, unit_one, scale_one, vectors[0])
    input_grad = grad_inputs.astype(jnp.bfloat16)
    grad_attn = jnp.concatenate([grad_w_qkv, grad_w_o[None]], 0)
    grad_gates = jnp.stack([grad_w_agate, grad_w_fgate])
    grad_vectors = jnp.stack(
        [
            grad_gain_one,
            grad_shift_one,
            grad_gain_two,
            grad_shift_two,
            jnp.sum(grad_agate, 0),
            jnp.sum(grad_fgate, 0),
            jnp.sum(grad_branch, 0),
        ]
    )
    grad_bias = jnp.sum(grad_hidden, 0)
    owned = (
        lax.psum_scatter(grad_attn, ("dp", "inner"), scatter_dimension=1, tiled=True),
        lax.psum_scatter(grad_gates, ("dp", "inner"), scatter_dimension=1, tiled=True),
        lax.psum_scatter(grad_w_in, ("dp", "inner"), scatter_dimension=0, tiled=True),
        lax.psum_scatter(grad_w_out, ("dp", "inner"), scatter_dimension=0, tiled=True),
        lax.psum_scatter(grad_vectors, ("dp", "inner"), scatter_dimension=1, tiled=True),
        lax.psum_scatter(grad_bias, ("dp", "inner"), scatter_dimension=0, tiled=True),
    )
    local_squares = sum((jnp.sum(element * element) for element in owned))
    grad_norm = jnp.sqrt(lax.psum(local_squares, ("dp", "inner")))
    factor = jnp.minimum(1.0, clip_norm / (grad_norm + 1e-06))
    states = (
        (attn_weight, attn_m, attn_v),
        (gate_weight, gate_m, gate_v),
        (in_weight, in_m, in_v),
        (out_weight, out_m, out_v),
        (norm_params, norm_m, norm_v),
        (in_bias, bias_m, bias_v),
    )
    step_rates = (learn_rate, learn_rate, learn_rate, learn_rate, vector_rate, vector_rate)
    updated = [
        adam_update(state[0], state[1], state[2], gradient, factor, step_rate)
        for state, gradient, step_rate in zip(states, owned, step_rates)
    ]
    return (
        layer_out,
        input_grad,
        grad_norm,
        updated[0][0],
        updated[0][1],
        updated[0][2],
        updated[1][0],
        updated[1][1],
        updated[1][2],
        updated[2][0],
        updated[2][1],
        updated[2][2],
        updated[3][0],
        updated[3][1],
        updated[3][2],
        updated[4][0],
        updated[4][1],
        updated[4][2],
        updated[5][0],
        updated[5][1],
        updated[5][2],
    )


def solution(mesh):
    return jax.shard_map(
        body,
        mesh=mesh,
        in_specs=(
            P(("dp", "inner"), None),
            P(("dp", "inner")),
            P(("dp", "inner")),
            P(("dp", "inner"), None),
            P(None, ("dp", "inner"), None),
            P(None, ("dp", "inner"), None),
            P(None, ("dp", "inner"), None),
            P(None, ("dp", "inner"), None),
            P(None, ("dp", "inner"), None),
            P(None, ("dp", "inner"), None),
            P(("dp", "inner"), None),
            P(("dp", "inner"), None),
            P(("dp", "inner"), None),
            P(("dp", "inner"), None),
            P(("dp", "inner"), None),
            P(("dp", "inner"), None),
            P(None, ("dp", "inner")),
            P(None, ("dp", "inner")),
            P(None, ("dp", "inner")),
            P(("dp", "inner")),
            P(("dp", "inner")),
            P(("dp", "inner")),
        ),
        out_specs=(
            P(("dp", "inner"), None),
            P(("dp", "inner"), None),
            P(),
            P(None, ("dp", "inner"), None),
            P(None, ("dp", "inner"), None),
            P(None, ("dp", "inner"), None),
            P(None, ("dp", "inner"), None),
            P(None, ("dp", "inner"), None),
            P(None, ("dp", "inner"), None),
            P(("dp", "inner"), None),
            P(("dp", "inner"), None),
            P(("dp", "inner"), None),
            P(("dp", "inner"), None),
            P(("dp", "inner"), None),
            P(("dp", "inner"), None),
            P(None, ("dp", "inner")),
            P(None, ("dp", "inner")),
            P(None, ("dp", "inner")),
            P(("dp", "inner")),
            P(("dp", "inner")),
            P(("dp", "inner")),
        ),
        check_vma=False,
    )
```

profile of v0, /device:TPU:12, one launch (start us, length us, event | category | flops | bytes accessed | tf_op | source)
XLA Modules:
  0.0 1210.4 jit_solution(3663491869928504730)
XLA Ops:
  17.4 41.7 %all-reduce = bf16[2048]{0:T(1024)(128)(2,1)S(1)} all-reduce(bf16[2048]{0:T(1024)(128)(2,1)S(1)} %dynamic-update-slice), channel_id=1, replica_groups=mesh['dp'=8,'inner'=4] {'dp','inner'}, use_global_device_ids=true, to_apply=%add | all-reduce | flops 2048 | bytes 8192
  59.1 29.3 %all-gather = bf16[32,16,7]{1,2,0:T(8,128)(2,1)S(1)} all-gather(bf16[1,16,7]{1,2,0:T(8,128)(2,1)S(1)} %convert_bitcast_fusion.1), channel_id=1, replica_groups=mesh['dp'=8,'inner'=4] {'dp','inner'}, dimensions={0}, use_global_device_ids=true | all-gather | bytes 7392 | tf_op jit(solution)/shard_map/all_gather | solution.py:46
  127.5 5.1 fusion.131
  133.1 49.7 %all-gather.10.cloned.1.call-done = bf16[512,2048]{1,0:T(8,128)(2,1)} async-done(((bf16[16,2048]{1,0:T(8,128)(2,1)}), bf16[512,2048]{1,0:T(8,128)(2,1)}) %all-gather.10.cloned.1.call-update) | async-done | bytes 2097168 | tf_op jit(solution)/shard_map/all_gather | solution.py:44
  182.8 7.2 fusion.142
  190.0 51.2 %all-gather.12.cloned.1.call-done = bf16[2048,512]{1,0:T(8,128)(2,1)} async-done(((bf16[64,512]{1,0:T(8,128)(2,1)}), bf16[2048,512]{1,0:T(8,128)(2,1)}) %all-gather.12.cloned.1.call-update) | async-done | bytes 2097168 | tf_op jit(solution)/shard_map/all_gather | solution.py:45
  241.2 6.5 fusion.86
  267.3 8.1 fusion.143
  275.3 29.8 %fusion.79 = bf16[8,64,512]{2,1,0:T(8,128)(2,1)} fusion(bf16[1024,8,64]{0,2,1:T(8,128)(2,1)} %bitcast.126, f32[8,512,1024]{2,1,0:T(8,128)} %fusion.143, f32[8,512,1024]{2,1,0:T(8,128)} %copy-done.1, f32[8,512]{1,0:T(8,128)S(1)} %log_add_fusion.1), kind=kOutput, calls=%fused_computation.102 | convolution fusion | flops 566498304 | bytes 35143680 | tf_op jit(solution)/shard_map/hqk,khe->qhe/dot_general | solution.py:113
  305.1 31.1 %fusion.13 = f32[8,64,1024]{2,1,0:T(8,128)} fusion(bf16[512,8,64]{0,2,1:T(8,128)(2,1)} %bitcast.137, f32[8,512,1024]{2,1,0:T(8,128)} %fusion.143, f32[8,512,1024]{2,1,0:T(8,128)} %copy-done.1, f32[8,512]{1,0:T(8,128)S(1)} %log_add_fusion.1), kind=kOutput, calls=%fused_computation.20 | convolution fusion | flops 566236160 | bytes 36192256 | tf_op jit(solution)/shard_map/hqk,qhe->khe/dot_general | solution.py:117
  336.2 9.5 fusion.144
  345.8 7.4 fusion.24
  361.6 37.1 %fusion.76 = bf16[8,64,512]{2,1,0:T(8,128)(2,1)} fusion(bf16[1024,8,64]{0,2,1:T(8,128)(2,1)S(1)} %bitcast.127, f32[8,512,1024]{2,1,0:T(8,128)} %fusion.144, f32[8,512,1024]{2,1,0:T(8,128)} %copy-done, f32[8,512]{1,0:T(8,128)S(1)} %log_add_fusion), kind=kOutput, calls=%fused_computation.101 | convolution fusion | flops 566498304 | bytes 35143680 | tf_op jit(solution)/shard_map/hqk,khe->qhe/dot_general | solution.py:113
  398.7 31.8 %add_convert_fusion.1 = bf16[8,64,1024]{2,1,0:T(8,128)(2,1)} fusion(f32[8,64,1024]{2,1,0:T(8,128)} %fusion.13, bf16[512,8,64]{0,2,1:T(8,128)(2,1)} %bitcast.135, f32[8,512,1024]{2,1,0:T(8,128)} %fusion.144, f32[8,512,1024]{2,1,0:T(8,128)} %copy-done, f32[8,512]{1,0:T(8,128)S(1)} %log_add_fusion), kind=kOutput, calls=%fused_computation.76 | convolution fusion | flops 567284736 | bytes 37240832 | tf_op jit(solution)/shard_map/hqk,qhe->khe/dot_general | solution.py:117
  450.9 5.4 copy.128
  461.7 6.7 fusion.66
  470.0 8.0 fusion.85
  478.0 40.1 %all-reduce.2 = f32[2048]{0:T(1024)S(1)} all-reduce(f32[2048]{0:T(1024)S(1)} %get-tuple-element.168), channel_id=7, replica_groups=mesh['dp'=8,'inner'=4] {'dp','inner'}, use_global_device_ids=true, to_apply=%region_32.33.clone | all-reduce | flops 2048 | bytes 16384
  519.4 34.3 %reduce-scatter.13.cloned.1.call-done = f32[16,7]{1,0:T(8,128)} async-done(((f32[512,7]{1,0:T(8,128)}), f32[16,7]{1,0:T(8,128)}) %reduce-scatter.13.cloned.1.call-update) | async-done | bytes 464
  555.1 169.7 %all-reduce.5.cloned.1.call-done = f32[4,512,512]{2,0,1:T(4,128)} async-done(((f32[4,512,512]{2,0,1:T(4,128)}), f32[4,512,512]{2,0,1:T(4,128)}) %all-reduce.5.cloned.1.call-update) | async-done | bytes 4194320
  727.0 110.1 %reduce-scatter.7.cloned.1.call-done = f32[2,16,512]{2,1,0:T(8,128)} async-done(((f32[2,512,512]{2,1,0:T(8,128)}), f32[2,16,512]{2,1,0:T(8,128)}) %reduce-scatter.7.cloned.1.call-update) | async-done | bytes 65552 | tf_op jit(solution)/shard_map/reduce_scatter | solution.py:279
  839.9 137.9 %reduce-scatter.9.cloned.1.call-done = f32[16,2048]{1,0:T(8,128)} async-done(((f32[512,2048]{1,0:T(8,128)}), f32[16,2048]{1,0:T(8,128)}) %reduce-scatter.9.cloned.1.call-update) | async-done | bytes 131088 | tf_op jit(solution)/shard_map/reduce_scatter | solution.py:280
  979.9 138.4 %reduce-scatter.11.cloned.1.call-done = f32[64,512]{1,0:T(8,128)} async-done(((f32[2048,512]{1,0:T(8,128)}), f32[64,512]{1,0:T(8,128)}) %reduce-scatter.11.cloned.1.call-update) | async-done | bytes 131088 | tf_op jit(solution)/shard_map/reduce_scatter | solution.py:281
  1125.6 67.5 %psum.7 = f32[]{:T(128)} all-reduce(f32[]{:T(128)S(6)} %add.297), channel_id=1, replica_groups=mesh['dp'=8,'inner'=4] {'dp','inner'}, use_global_device_ids=true, to_apply=%region_34.35 | all-reduce | flops 1 | bytes 8 | tf_op jit(solution)/shard_map/psum | solution.py:286
  (211 shorter events, 126.2 us)
Async XLA Ops:
  7.2 81.4 %copy-start.39 = (s32[1024]{0:T(1024)S(1)}, s32[1024]{0:T(1024)}, u32[]{:S(2)}) copy-start(s32[1024]{0:T(1024)} %param.24) | copy-start | bytes 12292
  7.2 81.4 %copy-start.40 = (s32[1024]{0:T(1024)S(1)}, s32[1024]{0:T(1024)}, u32[]{:S(2)}) copy-start(s32[1024]{0:T(1024)} %param.23) | copy-start | bytes 12292
  7.2 82.8 %all-gather.8.cloned.1.call-start = ((), (), s32[]{:S(2)}) async-start(), calls=%async_computation.5 | async-start | bytes 2162688 | tf_op jit(solution)/shard_map/all_gather | solution.py:42
  9.0 118.5 %all-gather.6.cloned.1.call-start = ((), (), s32[]{:S(2)}) async-start(), calls=%async_computation.4 | async-start | bytes 1081344 | tf_op jit(solution)/shard_map/all_gather | solution.py:43
  10.5 172.3 %all-gather.10.cloned.1.call-start = ((), (), s32[]{:S(2)}) async-start(), calls=%async_computation.6 | async-start | bytes 2162688 | tf_op jit(solution)/shard_map/all_gather | solution.py:44
  12.1 229.0 %all-gather.12.cloned.1.call-start = ((), (), s32[]{:S(2)}) async-start(), calls=%async_computation.7 | async-start | bytes 2162688 | tf_op jit(solution)/shard_map/all_gather | solution.py:45
  13.8 539.9 %reduce-scatter.13.cloned.1.call-start = ((), (), s32[]{:S(2)}) async-start(), calls=%async_computation.11 | async-start | bytes 270336
  88.6 367.8 %copy-start.42 = (f32[1,512]{1,0:T(1,128)}, f32[1,512]{1,0:T(1,128)S(1)}, u32[]{:S(2)}) copy-start(f32[1,512]{1,0:T(1,128)S(1)} %get-tuple-element.153) | copy-start | bytes 6148
  336.2 17.0 %slice-start = ((s8[16777216]{0:T(1024)(128)(4,1)}), s8[4194304]{0:T(1024)(128)(4,1)S(1)}, s32[]{:S(2)}) async-start(s8[16777216]{0:T(1024)(128)(4,1)} %bitcast.118), calls=%async_computation.13 | async-start | bytes 8388608
  336.2 17.0 %slice-start.1 = ((s8[16777216]{0:T(1024)(128)(4,1)}), s8[4194304]{0:T(1024)(128)(4,1)S(1)}, s32[]{:S(2)}) async-start(s8[16777216]{0:T(1024)(128)(4,1)} %bitcast.118), calls=%async_computation.14 | async-start | bytes 8388608
  336.2 17.0 %slice-start.2 = ((s8[16777216]{0:T(1024)(128)(4,1)}), s8[4194304]{0:T(1024)(128)(4,1)S(1)}, s32[]{:S(2)}) async-start(s8[16777216]{0:T(1024)(128)(4,1)} %bitcast.118), calls=%async_computation.15 | async-start | bytes 8388608
  446.2 278.6 %all-reduce.5.cloned.1.call-start = ((), (), s32[]{:S(2)}) async-start(), calls=%async_computation.12 | async-start | bytes 8388608
  456.4 380.8 %reduce-scatter.7.cloned.1.call-start = ((), (), s32[]{:S(2)}) async-start(), calls=%async_computation.8 | async-start | bytes 2162688 | tf_op jit(solution)/shard_map/reduce_scatter | solution.py:279
  461.5 516.3 %reduce-scatter.9.cloned.1.call-start = ((), (), s32[]{:S(2)}) async-start(), calls=%async_computation.9 | async-start | bytes 4325376 | tf_op jit(solution)/shard_map/reduce_scatter | solution.py:280
  468.4 649.9 %reduce-scatter.11.cloned.1.call-start = ((), (), s32[]{:S(2)}) async-start(), calls=%async_computation.10 | async-start | bytes 4325376 | tf_op jit(solution)/shard_map/reduce_scatter | solution.py:281
  478.0 643.9 %copy-start.3 = (f32[1024,512]{1,0:T(8,128)S(1)}, f32[1024,512]{1,0:T(8,128)}, u32[]{:S(2)}) copy-start(f32[1024,512]{1,0:T(8,128)} %get-tuple-element.164) | copy-start | bytes 6291460
  518.1 603.7 %copy-start.41 = (f32[2048]{0:T(1024)}, f32[2048]{0:T(1024)S(1)}, u32[]{:S(2)}) copy-start(f32[2048]{0:T(1024)S(1)} %all-reduce.2) | copy-start | bytes 24580
  1121.9 74.6 %copy-start.30 = (f32[4,16,512]{2,1,0:T(8,128)S(1)}, f32[4,16,512]{2,1,0:T(8,128)}, u32[]{:S(2)}) copy-start(f32[4,16,512]{2,1,0:T(8,128)} %param.26) | copy-start | bytes 393220
  1121.9 78.1 %copy-start.31 = (f32[64,512]{1,0:T(8,128)S(1)}, f32[64,512]{1,0:T(8,128)}, u32[]{:S(2)}) copy-start(f32[64,512]{1,0:T(8,128)} %param.35) | copy-start | bytes 393220
  1121.9 78.1 %copy-start.34 = (f32[64,512]{1,0:T(8,128)S(1)}, f32[64,512]{1,0:T(8,128)}, u32[]{:S(2)}) copy-start(f32[64,512]{1,0:T(8,128)} %reduce-scatter.11.cloned.1.call-done) | copy-start | bytes 393220
  1125.6 76.2 %copy-start.32 = (f32[16,2048]{1,0:T(8,128)S(1)}, f32[16,2048]{1,0:T(8,128)}, u32[]{:S(2)}) copy-start(f32[16,2048]{1,0:T(8,128)} %param.32) | copy-start | bytes 393220
  1125.6 76.2 %copy-start.33 = (f32[16,2048]{1,0:T(8,128)S(1)}, f32[16,2048]{1,0:T(8,128)}, u32[]{:S(2)}) copy-start(f32[16,2048]{1,0:T(8,128)} %reduce-scatter.9.cloned.1.call-done) | copy-start | bytes 393220
  1125.6 76.2 %copy-start.37 = (f32[16,2048]{1,0:T(8,128)S(1)}, f32[16,2048]{1,0:T(8,128)}, u32[]{:S(2)}) copy-start(f32[16,2048]{1,0:T(8,128)} %param.33) | copy-start | bytes 393220
  1125.6 76.2 %copy-start.38 = (f32[16,2048]{1,0:T(8,128)S(1)}, f32[16,2048]{1,0:T(8,128)}, u32[]{:S(2)}) copy-start(f32[16,2048]{1,0:T(8,128)} %param.34) | copy-start | bytes 393220
  (40 other events, 187.2 us)
Sparse Core Ops, SparseCore 0:
  11.5 56.6 all-gather.7
  71.7 52.8 all-gather.5
  128.0 54.7 all-gather.9
  186.1 55.0 all-gather.11
  446.3 107.3 reduce-scatter.12
  559.1 165.6 all-reduce.4
  727.1 109.9 reduce-scatter.6
  839.4 138.3 reduce-scatter.8
  980.0 138.3 reduce-scatter.10
where the time goes:
time: 1210 us
  waiting for transfers between devices  691 us (57%)
  matrix products  237 us (20%)
  blocking collectives  179 us (15%)
  other arithmetic  47.2 us (4%)
  local copies, waits for them, and re-layouts  34.7 us (3%)
  between operations  20.6 us (2%)
    unnamed x11, waiting for transfers between devices  204 us
    reduce_scatter x1, waiting for transfers between devices, body(): lax.psum_scatter(grad_w_out, ('dp', 'inner'), scatter_dimension=0, tiled=...  138 us
    reduce_scatter x1, waiting for transfers between devices, body(): lax.psum_scatter(grad_w_in, ('dp', 'inner'), scatter_dimension=0, tiled=T...  138 us
    reduce_scatter x1, waiting for transfers between devices, body(): lax.psum_scatter(grad_gates, ('dp', 'inner'), scatter_dimension=1, tiled=...  110 us
    unnamed x2, blocking collectives  81.8 us
    psum x1, blocking collectives, body(): grad_norm = jnp.sqrt(lax.psum(local_squares, ('dp', 'inner')))  67.5 us
    dot_general x2, matrix products, attend_back(): jnp.einsum('hqk,khe->qhe', grad_raw, key_heads, preferred_element_type=jn...  66.9 us
    dot_general x2, matrix products, attend_back(): jnp.einsum('hqk,qhe->khe', grad_raw, query_part, preferred_element_type=j...  62.9 us
  transfers between devices with their start and end apart: 9, of which 7 were waited for; matrix products, arithmetic and copies ran while one was open for 8% of the time, Pallas kernels for 0%

commit v1 on v0

--- a/solution.py
+++ b/solution.py
@@ -17,6 +17,27 @@
 masked_score = -1e30
 
 
+def in_order(blocks, dim):
+    shape = list(blocks.shape[1:])
+    shape[dim] *= blocks.shape[0]
+    return jnp.moveaxis(blocks, 0, dim).reshape(shape)
+
+
+def collected_by_bits(array, axis):
+    size, here = (lax.axis_size(axis), lax.axis_index(axis))
+    pieces, bit = (array[None], 1)
+    while bit < size:
+        other = lax.ppermute(pieces, axis, [(i, i ^ bit) for i in range(size)])
+        low = here & bit == 0
+        pieces = jnp.concatenate([jnp.where(low, pieces, other), jnp.where(low, other, pieces)])
+        bit *= 2
+    return pieces
+
+
+def gather_by_bits(shard, axis, dim):
+    return in_order(collected_by_bits(shard, axis), dim)
+
+
 def normalize_parts(values, gain_row, bias_row):
     centred = values - jnp.mean(values, -1, keepdims=True)
     spread = jnp.mean(centred * centred, -1, keepdims=True)
@@ -41,7 +62,7 @@
     return (
         lax.all_gather(low_attn, ("dp", "inner"), axis=1, tiled=True),
         lax.all_gather(low_gate, ("dp", "inner"), axis=1, tiled=True),
-        lax.all_gather(low_in, ("dp", "inner"), axis=0, tiled=True),
+        gather_by_bits(low_in, ("dp", "inner"), 0),
         lax.all_gather(low_out, ("dp", "inner"), axis=0, tiled=True),
         lax.all_gather(low_vec, ("dp", "inner"), axis=1, tiled=True),
         lax.all_gather(low_shift, ("dp", "inner"), axis=0, tiled=True),

time: 1210 us -> 1180 us (0.975)
  waiting for transfers between devices: 691 us -> 612 us
  blocking collectives: 179 us -> 214 us
    all_gather x1 -> x0, waiting for transfers between devices: 49.7 us -> none  [fetch(): lax.all_gather(low_in, ('dp', 'inner'), axis=0, tiled=True)]
    all_gather x1, waiting for transfers between devices: 51.2 us -> 9.9 us  [fetch(): lax.all_gather(low_out, ('dp', 'inner'), axis=0, tiled=True)]
    unnamed x2, blocking collectives: 81.8 us -> 109 us
    unnamed x11 -> x10, waiting for transfers between devices: 204 us -> 204 us
  transfers between devices with their start and end apart: 9 -> 13, of which waited for: 7 -> 9; matrix products, arithmetic and copies ran while one was open for 8% -> 8% of each run, Pallas kernels for 0% -> 0%
where the time goes in v1:
time: 1180 us
  waiting for transfers between devices  612 us (52%)
  matrix products  235 us (20%)
  blocking collectives  214 us (18%)
  other arithmetic  48.5 us (4%)
  local copies, waits for them, and re-layouts  36.3 us (3%)
  between operations  21 us (2%)
    unnamed x10, waiting for transfers between devices  204 us
    reduce_scatter x1, waiting for transfers between devices, body(): lax.psum_scatter(grad_w_out, ('dp', 'inner'), scatter_dimension=0, tiled=...  139 us
    reduce_scatter x1, waiting for transfers between devices, body(): lax.psum_scatter(grad_w_in, ('dp', 'inner'), scatter_dimension=0, tiled=T...  138 us
    reduce_scatter x1, waiting for transfers between devices, body(): lax.psum_scatter(grad_gates, ('dp', 'inner'), scatter_dimension=1, tiled=...  110 us
    unnamed x2, blocking collectives  109 us
    psum x1, blocking collectives, body(): grad_norm = jnp.sqrt(lax.psum(local_squares, ('dp', 'inner')))  67.5 us
    dot_general x2, matrix products, attend_back(): jnp.einsum('hqk,khe->qhe', grad_raw, key_heads, preferred_element_type=jn...  67.1 us
    dot_general x2, matrix products, attend_back(): jnp.einsum('hqk,qhe->khe', grad_raw, query_part, preferred_element_type=j...  62.9 us
  transfers between devices with their start and end apart: 13, of which 9 were waited for; matrix products, arithmetic and copies ran while one was open for 8% of the time, Pallas kernels for 0%

profile of v1, /device:TPU:12, one launch (start us, length us, event | category | flops | bytes accessed | tf_op | source)
XLA Modules:
  0.0 1175.3 jit_solution(3108032962207816453)
XLA Ops:
  20.2 7.2 collective-permute-done.2
  28.0 37.6 %all-gather = bf16[32,16,7]{1,2,0:T(8,128)(2,1)S(1)} all-gather(bf16[1,16,7]{1,2,0:T(8,128)(2,1)S(1)} %convert_bitcast_fusion.2), channel_id=1, replica_groups=mesh['dp'=8,'inner'=4] {'dp','inner'}, dimensions={0}, use_global_device_ids=true | all-gather | bytes 7392 | tf_op jit(solution)/shard_map/all_gather | solution.py:67
  67.5 6.4 collective-permute-start.4
  74.2 68.6 %all-reduce = bf16[2048]{0:T(1024)(128)(2,1)S(1)} all-reduce(bf16[2048]{0:T(1024)(128)(2,1)S(1)} %dynamic-update-slice), channel_id=1, replica_groups=mesh['dp'=8,'inner'=4] {'dp','inner'}, use_global_device_ids=true, to_apply=%add | all-reduce | flops 2048 | bytes 8192
  187.9 5.7 fusion.146
  193.6 9.9 all-gather.9.cloned.1.call-done
  203.5 6.5 fusion.89
  231.4 8.1 fusion.147
  239.5 29.8 %fusion.82 = bf16[8,64,512]{2,1,0:T(8,128)(2,1)} fusion(bf16[1024,8,64]{0,2,1:T(8,128)(2,1)} %bitcast.129, f32[8,512,1024]{2,1,0:T(8,128)} %fusion.147, f32[8,512,1024]{2,1,0:T(8,128)} %copy-done.1, f32[8,512]{1,0:T(8,128)S(1)} %log_add_fusion.1), kind=kOutput, calls=%fused_computation.103 | convolution fusion | flops 566498304 | bytes 35143680 | tf_op jit(solution)/shard_map/hqk,khe->qhe/dot_general | solution.py:134
  269.3 31.1 %fusion.13 = f32[8,64,1024]{2,1,0:T(8,128)} fusion(bf16[512,8,64]{0,2,1:T(8,128)(2,1)} %bitcast.142, f32[8,512,1024]{2,1,0:T(8,128)} %fusion.147, f32[8,512,1024]{2,1,0:T(8,128)} %copy-done.1, f32[8,512]{1,0:T(8,128)S(1)} %log_add_fusion.1), kind=kOutput, calls=%fused_computation.20 | convolution fusion | flops 566236160 | bytes 36192256 | tf_op jit(solution)/shard_map/hqk,qhe->khe/dot_general | solution.py:138
  300.4 9.5 fusion.148
  310.0 7.4 fusion.24
  325.7 37.3 %fusion.79 = bf16[8,64,512]{2,1,0:T(8,128)(2,1)} fusion(bf16[1024,8,64]{0,2,1:T(8,128)(2,1)S(1)} %bitcast.130, f32[8,512,1024]{2,1,0:T(8,128)} %fusion.148, f32[8,512,1024]{2,1,0:T(8,128)} %copy-done, f32[8,512]{1,0:T(8,128)S(1)} %log_add_fusion), kind=kOutput, calls=%fused_computation.102 | convolution fusion | flops 566498304 | bytes 35143680 | tf_op jit(solution)/shard_map/hqk,khe->qhe/dot_general | solution.py:134
  363.1 31.8 %add_convert_fusion.1 = bf16[8,64,1024]{2,1,0:T(8,128)(2,1)} fusion(f32[8,64,1024]{2,1,0:T(8,128)} %fusion.13, bf16[512,8,64]{0,2,1:T(8,128)(2,1)} %bitcast.140, f32[8,512,1024]{2,1,0:T(8,128)} %fusion.148, f32[8,512,1024]{2,1,0:T(8,128)} %copy-done, f32[8,512]{1,0:T(8,128)S(1)} %log_add_fusion), kind=kOutput, calls=%fused_computation.77 | convolution fusion | flops 567284736 | bytes 37240832 | tf_op jit(solution)/shard_map/hqk,qhe->khe/dot_general | solution.py:138
  415.2 5.4 copy.128
  426.0 6.7 fusion.66
  434.3 8.0 fusion.88
  442.3 40.1 %all-reduce.2 = f32[2048]{0:T(1024)S(1)} all-reduce(f32[2048]{0:T(1024)S(1)} %get-tuple-element.178), channel_id=7, replica_groups=mesh['dp'=8,'inner'=4] {'dp','inner'}, use_global_device_ids=true, to_apply=%region_32.33.clone | all-reduce | flops 2048 | bytes 16384
  483.7 34.3 %reduce-scatter.13.cloned.1.call-done = f32[16,7]{1,0:T(8,128)} async-done(((f32[512,7]{1,0:T(8,128)}), f32[16,7]{1,0:T(8,128)}) %reduce-scatter.13.cloned.1.call-update) | async-done | bytes 464
  519.4 169.8 %all-reduce.5.cloned.1.call-done = f32[4,512,512]{2,0,1:T(4,128)} async-done(((f32[4,512,512]{2,0,1:T(4,128)}), f32[4,512,512]{2,0,1:T(4,128)}) %all-reduce.5.cloned.1.call-update) | async-done | bytes 4194320
  691.3 110.2 %reduce-scatter.7.cloned.1.call-done = f32[2,16,512]{2,1,0:T(8,128)} async-done(((f32[2,512,512]{2,1,0:T(8,128)}), f32[2,16,512]{2,1,0:T(8,128)}) %reduce-scatter.7.cloned.1.call-update) | async-done | bytes 65552 | tf_op jit(solution)/shard_map/reduce_scatter | solution.py:300
  804.3 137.8 %reduce-scatter.9.cloned.1.call-done = f32[16,2048]{1,0:T(8,128)} async-done(((f32[512,2048]{1,0:T(8,128)}), f32[16,2048]{1,0:T(8,128)}) %reduce-scatter.9.cloned.1.call-update) | async-done | bytes 131088 | tf_op jit(solution)/shard_map/reduce_scatter | solution.py:301
  944.3 138.7 %reduce-scatter.11.cloned.1.call-done = f32[64,512]{1,0:T(8,128)} async-done(((f32[2048,512]{1,0:T(8,128)}), f32[64,512]{1,0:T(8,128)}) %reduce-scatter.11.cloned.1.call-update) | async-done | bytes 131088 | tf_op jit(solution)/shard_map/reduce_scatter | solution.py:302
  1090.2 67.5 %psum.7 = f32[]{:T(128)} all-reduce(f32[]{:T(128)S(6)} %add.302), channel_id=1, replica_groups=mesh['dp'=8,'inner'=4] {'dp','inner'}, use_global_device_ids=true, to_apply=%region_34.35 | all-reduce | flops 1 | bytes 8 | tf_op jit(solution)/shard_map/psum | solution.py:307
  (240 shorter events, 139.1 us)
Async XLA Ops:
  7.2 139.1 %all-gather.7.cloned.1.call-start = ((), (), s32[]{:S(2)}) async-start(), calls=%async_computation.5 | async-start | bytes 2162688 | tf_op jit(solution)/shard_map/all_gather | solution.py:63
  9.0 172.2 %all-gather.5.cloned.1.call-start = ((), (), s32[]{:S(2)}) async-start(), calls=%async_computation.4 | async-start | bytes 1081344 | tf_op jit(solution)/shard_map/all_gather | solution.py:64
  10.5 193.0 %all-gather.9.cloned.1.call-start = ((), (), s32[]{:S(2)}) async-start(), calls=%async_computation.6 | async-start | bytes 2162688 | tf_op jit(solution)/shard_map/all_gather | solution.py:66
  11.5 1.3 collective-permute-start
  13.7 5.6 collective-permute-start.1
  16.8 501.2 %reduce-scatter.13.cloned.1.call-start = ((), (), s32[]{:S(2)}) async-start(), calls=%async_computation.10 | async-start | bytes 270336
  19.4 8.0 collective-permute-start.2
  27.5 38.9 %collective-permute-start.3 = (bf16[8,16,2048]{2,1,0:T(8,128)(2,1)S(1)}, bf16[8,16,2048]{2,1,0:T(8,128)(2,1)S(1)}, u32[]{:S(2)}, u32[]{:S(2)}) collective-permute-start(bf16[8,16,2048]{2,1,0:T(8,128)(2,1)S(1)} %pad_maximum_fusion.10), channel_id=1, source_target_pairs={{0,8},{1,9},{2,10},{3,11},{4,12},{5,13},{6,14},{7,15},{8,0},{9,1},... | collective-permute-start | bytes 1572872 | tf_op jit(solution)/shard_map/ppermute | solution.py:30
  66.3 76.4 %copy-start.44 = (s32[1024]{0:T(1024)S(1)}, s32[1024]{0:T(1024)}, u32[]{:S(2)}) copy-start(s32[1024]{0:T(1024)} %param.24) | copy-start | bytes 12292
  66.4 76.4 %copy-start.45 = (s32[1024]{0:T(1024)S(1)}, s32[1024]{0:T(1024)}, u32[]{:S(2)}) copy-start(s32[1024]{0:T(1024)} %param.23) | copy-start | bytes 12292
  67.5 77.1 %collective-permute-start.4 = (bf16[16,16,2048]{2,1,0:T(8,128)(2,1)}, bf16[16,16,2048]{2,1,0:T(8,128)(2,1)S(1)}, u32[]{:S(2)}, u32[]{:S(2)}) collective-permute-start(bf16[16,16,2048]{2,1,0:T(8,128)(2,1)} %pad_maximum_fusion.7), channel_id=1, source_target_pairs={{0,16},{1,17},{2,18},{3,19},{4,20},{5,21},{6,22},{7,23},{8,24},{9,... | collective-permute-start | bytes 3145736 | tf_op jit(solution)/shard_map/ppermute | solution.py:30
  142.8 277.9 %copy-start.48 = (f32[1,512]{1,0:T(1,128)}, f32[1,512]{1,0:T(1,128)S(1)}, u32[]{:S(2)}) copy-start(f32[1,512]{1,0:T(1,128)S(1)} %get-tuple-element.163) | copy-start | bytes 6148
  410.5 278.6 %all-reduce.5.cloned.1.call-start = ((), (), s32[]{:S(2)}) async-start(), calls=%async_computation.11 | async-start | bytes 8388608
  420.7 380.8 %reduce-scatter.7.cloned.1.call-start = ((), (), s32[]{:S(2)}) async-start(), calls=%async_computation.7 | async-start | bytes 2162688 | tf_op jit(solution)/shard_map/reduce_scatter | solution.py:300
  425.8 516.2 %reduce-scatter.9.cloned.1.call-start = ((), (), s32[]{:S(2)}) async-start(), calls=%async_computation.8 | async-start | bytes 4325376 | tf_op jit(solution)/shard_map/reduce_scatter | solution.py:301
  432.8 650.2 %reduce-scatter.11.cloned.1.call-start = ((), (), s32[]{:S(2)}) async-start(), calls=%async_computation.9 | async-start | bytes 4325376 | tf_op jit(solution)/shard_map/reduce_scatter | solution.py:302
  442.3 644.1 %copy-start.3 = (f32[1024,512]{1,0:T(8,128)S(1)}, f32[1024,512]{1,0:T(8,128)}, u32[]{:S(2)}) copy-start(f32[1024,512]{1,0:T(8,128)} %get-tuple-element.174) | copy-start | bytes 6291460
  482.4 604.0 %copy-start.47 = (f32[2048]{0:T(1024)}, f32[2048]{0:T(1024)S(1)}, u32[]{:S(2)}) copy-start(f32[2048]{0:T(1024)S(1)} %all-reduce.2) | copy-start | bytes 24580
  1086.5 78.1 %copy-start.37 = (f32[64,512]{1,0:T(8,128)S(1)}, f32[64,512]{1,0:T(8,128)}, u32[]{:S(2)}) copy-start(f32[64,512]{1,0:T(8,128)} %param.35) | copy-start | bytes 393220
  1086.5 78.1 %copy-start.39 = (f32[64,512]{1,0:T(8,128)S(1)}, f32[64,512]{1,0:T(8,128)}, u32[]{:S(2)}) copy-start(f32[64,512]{1,0:T(8,128)} %reduce-scatter.11.cloned.1.call-done) | copy-start | bytes 393220
  1090.2 76.2 %copy-start.27 = (f32[16,2048]{1,0:T(8,128)S(1)}, f32[16,2048]{1,0:T(8,128)}, u32[]{:S(2)}) copy-start(f32[16,2048]{1,0:T(8,128)} %param.32) | copy-start | bytes 393220
  1090.2 76.2 %copy-start.38 = (f32[16,2048]{1,0:T(8,128)S(1)}, f32[16,2048]{1,0:T(8,128)}, u32[]{:S(2)}) copy-start(f32[16,2048]{1,0:T(8,128)} %reduce-scatter.9.cloned.1.call-done) | copy-start | bytes 393220
  1090.2 76.2 %copy-start.42 = (f32[16,2048]{1,0:T(8,128)S(1)}, f32[16,2048]{1,0:T(8,128)}, u32[]{:S(2)}) copy-start(f32[16,2048]{1,0:T(8,128)} %param.33) | copy-start | bytes 393220
  1090.2 76.2 %copy-start.43 = (f32[16,2048]{1,0:T(8,128)S(1)}, f32[16,2048]{1,0:T(8,128)}, u32[]{:S(2)}) copy-start(f32[16,2048]{1,0:T(8,128)} %param.34) | copy-start | bytes 393220
  (50 other events, 350.6 us)
Sparse Core Ops, SparseCore 0:
  11.4 56.6 all-gather.6
  71.6 73.6 all-gather.4
  148.7 54.7 all-gather.8
  410.7 107.3 reduce-scatter.12
  523.4 165.7 all-reduce.4
  691.3 110.1 reduce-scatter.6
  803.8 138.2 reduce-scatter.8
  944.3 138.5 reduce-scatter.10
